TPU v7x, 32 devices: a whole 2x2x4 slice. The times are simulated.
32 devices in a mesh: dp: 2 (over x), space: 16 (over z, y, core).
Axes of the slice: x: 2, y: 2, z: 4, core: 2. Of those that a mesh axis runs over, the one named last changes fastest.
Arguments:
- stash: bfloat16 [16, 16, 4, 8640], P('space', None, 'dp'), may hold values from -5 to 5
- piece_map: int32 [16, 16], P(None, 'space'), may hold values from 0 to 15, as said below
- gain_one: float32 [768], replicated, may hold values from 0.5 to 1.5
- spec_one: float32 [2, 8, 96, 96], replicated, may hold values from -0.4375 to 0.4375
- bias_one: float32 [2, 768], replicated, may hold values from -3 to 3
- spec_two: float32 [2, 8, 96, 96], replicated, may hold values from -0.4375 to 0.4375
- bias_two: float32 [2, 768], replicated, may hold values from -0.6 to 0.6
- gain_two: float32 [768], replicated, may hold values from 0.5 to 1.5
- fc_one: bfloat16 [768, 3072], replicated, may hold values from -0.21875 to 0.21875
- bias_fc: float32 [3072], replicated, may hold values from -3 to 3
- fc_two: bfloat16 [3072, 768], replicated, may hold values from -0.109375 to 0.109375
- cotangent: bfloat16 [4, 16, 180, 768], P('dp', 'space'), may hold values from -6 to 6
Outputs:
- grad_input: float32 [4, 16, 180, 768], P('dp', 'space')
- grad_fc_one: float32 [768, 3072], P(None, ('dp', 'space'))
- grad_fc_two: float32 [3072, 768], P(('dp', 'space'))
- grad_bias_fc: float32 [3072], replicated
- grad_bias_out: float32 [768], replicated
- grad_gain_one: float32 [768], replicated
- grad_gain_two: float32 [768], replicated
- grad_spec_one: float32 [2, 8, 96, 96], replicated
- grad_bias_one: float32 [2, 768], replicated
- grad_spec_two: float32 [2, 8, 96, 96], replicated
- grad_bias_two: float32 [2, 768], replicated
Inputs may be any that keep to these rules, and one draw needn't show every extreme that they name: `piece_map`: each column holds every number from 0 to 15 once.
All inputs are finite; a program needn't handle non-finite values.
Results may differ from a plain program's by a relative error of at most 0.0046.
Values may be sent and summed in bfloat16 or wider, within the bound.
A program may use at most 128 MiB of HBM per device.

v0:
```python
import math
import jax
import jax.numpy as jnp
import numpy as np
from jax import lax
from jax.sharding import PartitionSpec as P

KW = 64
epsilon = 1e-05
high = lax.Precision.HIGH
everyone = ("dp", "space")


def layer_norm(values, gain_vector):
    centred = values - jnp.mean(values, axis=-1, keepdims=True)
    spread = jnp.mean(centred * centred, axis=-1, keepdims=True)
    return centred * lax.rsqrt(spread + epsilon) * gain_vector


def smooth_gate(values):
    return jax.nn.gelu(values, approximate=True)


def complex_blocks(weights):
    top = jnp.concatenate((weights[0], weights[1]), axis=2)
    bottom = jnp.concatenate((-weights[1], weights[0]), axis=2)
    return jnp.concatenate((top, bottom), axis=1)


def complex_bias(biases, blocks):
    return biases.reshape(2, blocks, 1, -1).transpose(1, 2, 0, 3).reshape(blocks, 1, -1)


def block_dot(values, weights):
    return jnp.einsum("nri,nio->nro", values, weights, precision=high)


def spectral_mlp(spectrum, spec_one, bias_one, spec_two, bias_two):
    blocks = spec_one.shape[1]
    inner = block_dot(spectrum, complex_blocks(spec_one)) + complex_bias(bias_one, blocks)
    return block_dot(smooth_gate(inner), complex_blocks(spec_two)) + complex_bias(bias_two, blocks)


def zonal_tables(length, ranks):
    positions = np.arange(length)[:, None]
    frequency = np.arange(KW)[None, :]
    angles = positions * frequency % length * (2.0 * math.pi / length)
    table = np.stack((np.cos(angles), -np.sin(angles))) / math.sqrt(length)
    doubled = table * np.where(frequency == 0, 1.0, 2.0)
    shaped = [
        item.reshape(2, length, ranks, KW // ranks).transpose(1, 2, 0, 3).astype(np.float32)
        for item in (table, doubled)
    ]
    return shaped


def meridian_table(length, ranks):
    positions = np.arange(length)
    angles = positions[:, None] * positions[None, :] % length * (2.0 * math.pi / length)
    cosine = np.cos(angles) / math.sqrt(length)
    sine = np.sin(angles) / math.sqrt(length)
    table = np.stack((np.stack((cosine, -sine), -1), np.stack((sine, cosine), -1)), 1)
    return table.reshape(ranks, length // ranks, 2, length, 2).astype(np.float32)


def swap(pieces):
    return lax.all_to_all(pieces, "space", split_axis=0, concat_axis=0, tiled=True)


def to_modes(field, zonal, merid, blocks, carried):
    pieces = jnp.einsum("brwd,wscm->sbrcmd", field, zonal, precision=high)
    modes = swap(pieces.astype(carried)).astype(jnp.float32)
    spectrum = jnp.einsum("lbrcmd,lrcke->bmked", modes, merid, precision=high)
    rows = math.prod(spectrum.shape[:3])
    split = spectrum.reshape(rows, 2, blocks, -1)
    return split.transpose(2, 0, 1, 3).reshape(blocks, rows, -1)


def from_modes(spectrum, zonal, merid, samples, width, carried):
    blocks, rows = spectrum.shape[:2]
    length = merid.shape[3]
    split = spectrum.reshape(blocks, rows, 2, -1).transpose(1, 2, 0, 3)
    shaped = split.reshape(samples, rows // (samples * length), length, 2, width)
    pieces = jnp.einsum("bmked,lrcke->lbrcmd", shaped, merid, precision=high)
    modes = swap(pieces.astype(carried)).astype(jnp.float32)
    return jnp.einsum("sbrcmd,wscm->brwd", modes, zonal, precision=high)


def local(
    stash,
    piece_map,
    gain_one,
    spec_one,
    bias_one,
    spec_two,
    bias_two,
    gain_two,
    fc_one,
    bias_fc,
    fc_two,
    cotangent,
):
    samples, lat_rows, lon_cells, model_width = cotangent.shape
    space_ranks = lax.axis_size("space")
    lat_total = lat_rows * space_ranks
    tokens = samples * lat_rows * lon_cells
    blocks = spec_one.shape[1]
    arrived = lax.all_to_all(stash, "space", split_axis=1, concat_axis=0, tiled=True)
    ordering = jnp.argsort(piece_map[:, 0])
    placed = jnp.take(arrived[:, 0], ordering, axis=0)
    inputs = jnp.transpose(placed, (1, 0, 2)).reshape(samples, lat_rows, lon_cells, model_width)
    base_field = inputs.astype(jnp.float32)
    zonal, zonal_back = zonal_tables(lon_cells, space_ranks)
    merid = meridian_table(lat_total, space_ranks)
    normed, pull_one = jax.vjp(layer_norm, base_field, gain_one)
    spectrum = to_modes(normed, zonal, merid, blocks, jnp.float32)
    mixed_spec, pull_mix = jax.vjp(spectral_mlp, spectrum, spec_one, bias_one, spec_two, bias_two)
    spatial = from_modes(mixed_spec, zonal_back, merid, samples, model_width, jnp.float32)
    mixed_field = base_field + normed + spatial
    normed_two, pull_two = jax.vjp(layer_norm, mixed_field, gain_two)
    normed_flat = normed_two.astype(jnp.bfloat16).reshape(tokens, model_width)
    hidden_pre = jnp.dot(normed_flat, fc_one, preferred_element_type=jnp.float32) + bias_fc
    active, pull_gate = jax.vjp(smooth_gate, hidden_pre)
    active_flat = active.astype(jnp.bfloat16)
    upstream = cotangent.reshape(tokens, model_width)
    term_two = jnp.einsum("tf,td->fd", active_flat, upstream, preferred_element_type=jnp.float32)
    part_two = lax.psum_scatter(
        term_two.astype(jnp.bfloat16), everyone, scatter_dimension=0, tiled=True
    )
    grad_active = jnp.einsum("td,fd->tf", upstream, fc_two, preferred_element_type=jnp.float32)
    grad_hidden = pull_gate(grad_active)[0]
    grad_hidden_flat = grad_hidden.astype(jnp.bfloat16)
    term_one = jnp.einsum(
        "tf,td->fd", grad_hidden_flat, normed_flat, preferred_element_type=jnp.float32
    )
    part_one = lax.psum_scatter(
        term_one.astype(jnp.bfloat16), everyone, scatter_dimension=0, tiled=True
    )
    grad_normed_two = jnp.einsum(
        "tf,df->td", grad_hidden_flat, fc_one, preferred_element_type=jnp.float32
    )
    grad_mixed_norm, grad_gain_two = pull_two(grad_normed_two.reshape(mixed_field.shape))
    grad_mixed = cotangent.astype(jnp.float32) + grad_mixed_norm
    grad_spectrum = to_modes(grad_mixed, zonal_back, merid, blocks, jnp.bfloat16)
    pulled = pull_mix(grad_spectrum)
    grad_normed = grad_mixed + from_modes(
        pulled[0], zonal, merid, samples, model_width, jnp.bfloat16
    )
    grad_base, grad_gain_one = pull_one(grad_normed)
    grad_input = grad_mixed + grad_base
    bias_sum = jnp.sum(grad_hidden, axis=0)
    out_sum = jnp.sum(cotangent, axis=(0, 1, 2), dtype=jnp.float32)
    totals = lax.psum(
        (
            grad_gain_one,
            grad_gain_two,
            pulled[1],
            pulled[2],
            pulled[3],
            pulled[4],
            bias_sum,
            out_sum,
        ),
        everyone,
    )
    grad_scale = 1.0 / math.sqrt(samples * lax.axis_size("dp") * lat_total * lon_cells)
    return (
        grad_input,
        (part_one.astype(jnp.float32) * grad_scale).T,
        part_two.astype(jnp.float32) * grad_scale,
        totals[6] * grad_scale,
        totals[7] * grad_scale,
        totals[0] * grad_scale,
        totals[1] * grad_scale,
        totals[2] * grad_scale,
        totals[3] * grad_scale,
        totals[4] * grad_scale,
        totals[5] * grad_scale,
    )


def solution(mesh):
    placed = (
        P("space", None, "dp", None),
        P(None, "space"),
        P(),
        P(),
        P(),
        P(),
        P(),
        P(),
        P(),
        P(),
        P(),
        P("dp", "space", None, None),
    )
    return jax.shard_map(
        local,
        mesh=mesh,
        in_specs=placed,
        out_specs=(
            P("dp", "space", None, None),
            P(None, ("dp", "space")),
            P(("dp", "space"), None),
            P(),
            P(),
            P(),
            P(),
            P(),
            P(),
            P(),
            P(),
        ),
        check_vma=False,
    )
```

profile of v0, /device:TPU:0, one launch (start us, length us, event | category | flops | bytes accessed | tf_op | source)
XLA Modules:
  0.0 514.6 jit_solution(12274644097293364253)
XLA Ops:
  7.2 7.4 %all-to-all-start = ((bf16[1,16,2,8640]{3,2,0,1:T(2,128)(2,1)}), bf16[1,16,2,8640]{3,2,0,1:T(2,128)(2,1)S(1)}, u32[]{:S(2)}, u32[]{:S(2)}) async-start(bf16[1,16,2,8640]{3,2,0,1:T(2,128)(2,1)} %bitcast.227), calls=%async_computation | async-start | bytes 1114112 | tf_op jit(solution)/shard_map/all_to_all | solution.py:108
  14.6 1.9 sort.17
  16.5 12.9 %all-to-all-done = bf16[1,16,2,8640]{3,2,0,1:T(2,128)(2,1)S(1)} async-done(((bf16[1,16,2,8640]{3,2,0,1:T(2,128)(2,1)}), bf16[1,16,2,8640]{3,2,0,1:T(2,128)(2,1)S(1)}, u32[]{:S(2)}, u32[]{:S(2)}) %all-to-all-start) | async-done | bytes 552992 | tf_op jit(solution)/shard_map/all_to_all | solution.py:108
  29.4 1.7 gather_fusion
  35.0 1.5 copy.105
  36.5 4.8 all-to-all-start.1
  41.9 0.9 copy.158
  42.8 1.9 fusion.71
  44.7 1.2 copy.161
  45.9 0.9 copy.160
  48.4 11.5 %all-to-all-done.1 = f32[16,2,1,2,4,768]{5,1,4,3,2,0:T(2,128)S(1)} async-done(((f32[16,2,1,2,4,768]{5,1,4,3,2,0:T(2,128)}), f32[16,2,1,2,4,768]{5,1,4,3,2,0:T(2,128)S(1)}, u32[]{:S(2)}, u32[]{:S(2)}) %all-to-all-start.1) | async-done | bytes 786464 | tf_op jit(solution)/shard_map/all_to_all | solution.py:67
  61.8 2.6 convolution_add_fusion.2
  64.4 1.4 convolution_add_fusion.1
  67.5 1.4 copy.118
  68.9 5.6 %all-to-all-start.2 = ((f32[16,2,1,2,4,768]{5,4,1,3,2,0:T(4,128)}), f32[16,2,1,2,4,768]{5,4,1,3,2,0:T(4,128)}, u32[]{:S(2)}, u32[]{:S(2)}) async-start(f32[16,2,1,2,4,768]{5,4,1,3,2,0:T(4,128)} %copy.118), calls=%async_computation.2 | async-start | bytes 1572864 | tf_op jit(solution)/shard_map/all_to_all | solution.py:67
  75.3 6.7 %fusion.75 = f32[360,3072]{1,0:T(8,128)} fusion(bf16[360,768]{1,0:T(8,128)(2,1)S(1)} %reshape.326, bf16[3072,768]{1,0:T(8,128)(2,1)} %param.30), kind=kOutput, calls=%fused_computation.144 | convolution fusion | flops 1698693120 | bytes 9695232 | tf_op jit(solution)/shard_map/td,fd->tf/dot_general | solution.py:130
  81.9 11.3 %all-to-all-done.2 = f32[16,2,1,2,4,768]{5,4,1,3,2,0:T(4,128)} async-done(((f32[16,2,1,2,4,768]{5,4,1,3,2,0:T(4,128)}), f32[16,2,1,2,4,768]{5,4,1,3,2,0:T(4,128)}, u32[]{:S(2)}, u32[]{:S(2)}) %all-to-all-start.2) | async-done | bytes 786464 | tf_op jit(solution)/shard_map/all_to_all | solution.py:67
  93.2 2.4 fusion.73
  97.0 9.6 %fusion.68 = (f32[3072]{0:T(1024)S(1)}, bf16[360,3072]{1,0:T(8,128)(2,1)S(1)}, f32[360,3072]{1,0:T(8,128)}) fusion(f32[360,3072]{1,0:T(8,128)} %fusion.75, f32[3072]{0:T(1024)S(1)} %copy-done.27, bf16[360,768]{1,0:T(8,128)(2,1)S(1)} %reshape.337, bf16[768,3072]{1,0:T(8,128)(2,1)} %param.28), kind=kOutput, calls=%fused_computation.138 | convolution fusion | flops 1723020288 | bytes 16355328 | tf_op jit(solution)/shard_map/dot_general | solution.py:122
  106.6 1.4 copy-done.30
  108.1 5.2 %fusion.23 = f32[360,768]{1,0:T(8,128)} fusion(bf16[768,3072]{1,0:T(8,128)(2,1)} %param.28, bf16[360,3072]{1,0:T(8,128)(2,1)S(1)} %get-tuple-element.70), kind=kOutput, calls=%fused_computation.58 | convolution fusion | flops 1698693120 | bytes 8036352 | tf_op jit(solution)/shard_map/tf,df->td/dot_general | solution.py:139
  113.3 1.4 reshape.338
  115.7 1.7 fusion.70
  118.3 17.5 %all_to_all.29 = bf16[16,2,1,2,4,768]{5,4,3,1,2,0:T(4,128)(2,1)S(1)} all-to-all(bf16[16,2,1,2,4,768]{5,4,3,1,2,0:T(4,128)(2,1)S(1)} %copy.120), channel_id=1, replica_groups=mesh['dp'=2,'space'=16] {'space'}, dimensions={0} | all-to-all | bytes 786432 | tf_op jit(solution)/shard_map/all_to_all | solution.py:67
  136.3 0.9 copy.122
  137.2 1.6 reshape.342
  138.8 1.3 copy.123
  140.1 4.4 fusion.74
  144.5 0.9 fusion.47
  147.7 1.0 pad_add_fusion
  148.7 1.0 pad_add_fusion.1
  149.7 6.5 %convolution_convert_fusion.1 = bf16[3072,768]{1,0:T(8,128)(2,1)} fusion(bf16[360,768]{1,0:T(8,128)(2,1)} %copy-done.15, bf16[360,3072]{1,0:T(8,128)(2,1)} %copy-done.30), kind=kOutput, calls=%fused_computation.4 | convolution fusion | flops 1701052416 | bytes 7483392 | tf_op jit(solution)/shard_map/tf,td->fd/dot_general | solution.py:133
  156.5 7.6 %convolution_convert_fusion = bf16[3072,768]{1,0:T(8,128)(2,1)} fusion(bf16[360,768]{1,0:T(8,128)(2,1)} %copy-done.14, f32[360,3072]{1,0:T(8,128)} %get-tuple-element.89), kind=kOutput, calls=%fused_computation.3 | convolution fusion | flops 1711005696 | bytes 9695232 | tf_op jit(solution)/shard_map/tf,td->fd/dot_general | solution.py:126
  164.1 4.6 fusion.21
  168.7 2.4 copy.126
  171.1 2.5 reshape.345
  173.6 1.7 fusion.14
  175.3 1.0 copy.129
  176.3 4.2 all-to-all-start.4
  180.9 100.9 %all-reduce.12.cloned.1.call-done = (f32[2,8,96,96]{3,2,1,0:T(8,128)}, f32[2,8,96,96]{3,2,1,0:T(8,128)}) async-done(((f32[2,8,96,96]{3,2,1,0:T(8,128)}, f32[2,8,96,96]{3,2,1,0:T(8,128)}), (f32[2,8,96,96]{3,2,1,0:T(8,128)}, f32[2,8,96,96]{3,2,1,0:T(8,128)})) %all-reduce.12.cloned.1.call-update) | async-done | bytes 1179664 | tf_op jit(solution)/shard_map/psum | solution.py:153
  281.8 2.7 broadcast_multiply_fusion
  284.6 2.0 multiply_reduce_fusion.2
  287.7 2.1 copy.132
  289.8 39.8 %all-reduce.8 = (f32[3072]{0:T(1024)S(1)}, f32[768]{0:T(1024)S(1)}, f32[768]{0:T(1024)S(1)}, f32[768]{0:T(1024)S(1)}, f32[2,768]{1,0:T(2,128)S(1)}, /*index=5*/f32[2,768]{1,0:T(2,128)S(1)}) all-reduce(f32[3072]{0:T(1024)S(1)} %get-tuple-element.69, ...), channel_id=1, replica_groups=mesh['dp'=2,'space'=16] {'dp','space'}, use_global_device_ids=true, to_apply=%region_12.13 | all-reduce | flops 8448 | bytes 67584 | tf_op jit(solution)/shard_map/psum | solution.py:153
  332.0 62.0 %reduce-scatter.3.cloned.1.call-done = bf16[96,768]{1,0:T(8,128)(2,1)} async-done(((bf16[3072,768]{1,0:T(8,128)(2,1)}), bf16[96,768]{1,0:T(8,128)(2,1)}) %reduce-scatter.3.cloned.1.call-update) | async-done | bytes 147472 | tf_op jit(solution)/shard_map/reduce_scatter | solution.py:136
  394.0 1.6 multiply_bitcast_fusion
  395.7 110.6 %reduce-scatter.5.cloned.1.call-done = bf16[96,768]{1,0:T(8,128)(2,1)} async-done(((bf16[3072,768]{1,0:T(8,128)(2,1)}), bf16[96,768]{1,0:T(8,128)(2,1)}) %reduce-scatter.5.cloned.1.call-update) | async-done | bytes 147472 | tf_op jit(solution)/shard_map/reduce_scatter | solution.py:127
  506.2 1.6 convert_multiply_fusion
  (127 shorter events, 20.5 us)
Async XLA Ops:
  7.2 22.2 %all-to-all-start = ((bf16[1,16,2,8640]{3,2,0,1:T(2,128)(2,1)}), bf16[1,16,2,8640]{3,2,0,1:T(2,128)(2,1)S(1)}, u32[]{:S(2)}, u32[]{:S(2)}) async-start(bf16[1,16,2,8640]{3,2,0,1:T(2,128)(2,1)} %bitcast.227), calls=%async_computation | async-start | bytes 1114112 | tf_op jit(solution)/shard_map/all_to_all | solution.py:108
  33.4 0.9 copy-start.19
  33.4 0.9 copy-start.22
  36.5 4.8 copy-start.25
  36.5 5.0 copy-start.26
  36.5 5.1 copy-start.10
  36.5 23.4 %all-to-all-start.1 = ((f32[16,2,1,2,4,768]{5,1,4,3,2,0:T(2,128)}), f32[16,2,1,2,4,768]{5,1,4,3,2,0:T(2,128)S(1)}, u32[]{:S(2)}, u32[]{:S(2)}) async-start(f32[16,2,1,2,4,768]{5,1,4,3,2,0:T(2,128)} %copy.105), calls=%async_computation.1 | async-start | bytes 1572864 | tf_op jit(solution)/shard_map/all_to_all | solution.py:67
  41.8 19.9 %copy-start.7 = (f32[1,8,96,96]{2,3,1,0:T(8,128)}, f32[1,8,96,96]{2,3,1,0:T(8,128)S(1)}, u32[]{:S(2)}) copy-start(f32[1,8,96,96]{2,3,1,0:T(8,128)S(1)} %copy.159) | copy-start | bytes 884740
  45.9 2.5 copy-start.8
  45.9 14.0 %copy-start.20 = (f32[16,2,16,2,1,1]{0,2,1,3,5,4:T(8,128)S(1)}, f32[16,2,16,2,1,1]{0,2,1,3,5,4:T(8,128)}, u32[]{:S(2)}) copy-start(f32[16,2,16,2,1,1]{0,2,1,3,5,4:T(8,128)} %constant.86) | copy-start | bytes 12292
  61.8 2.6 copy-start.4
  61.8 2.6 copy-start.9
  61.8 2.6 copy-start.16
  61.8 2.6 copy-start.17
  64.4 1.4 copy-start.11
  66.2 0.8 copy-start.24
  68.9 6.2 %copy-start.1 = (bf16[2,1,180,768]{3,0,2,1:T(2,128)(2,1)S(1)}, bf16[2,1,180,768]{3,0,2,1:T(2,128)(2,1)}, u32[]{:S(2)}) copy-start(bf16[2,1,180,768]{3,0,2,1:T(2,128)(2,1)} %param.31) | copy-start | bytes 1658884
  68.9 24.3 %all-to-all-start.2 = ((f32[16,2,1,2,4,768]{5,4,1,3,2,0:T(4,128)}), f32[16,2,1,2,4,768]{5,4,1,3,2,0:T(4,128)}, u32[]{:S(2)}, u32[]{:S(2)}) async-start(f32[16,2,1,2,4,768]{5,4,1,3,2,0:T(4,128)} %copy.118), calls=%async_computation.2 | async-start | bytes 1572864 | tf_op jit(solution)/shard_map/all_to_all | solution.py:67
  74.5 207.4 %all-reduce.12.cloned.1.call-start = ((), (), s32[]{:S(2)}) async-start(), calls=%async_computation.9 | async-start | bytes 3145728 | tf_op jit(solution)/shard_map/psum | solution.py:153
  75.2 6.7 %copy-start.14 = (bf16[360,768]{1,0:T(8,128)(2,1)}, bf16[360,768]{1,0:T(8,128)(2,1)S(1)}, u32[]{:S(2)}) copy-start(bf16[360,768]{1,0:T(8,128)(2,1)S(1)} %reshape.326) | copy-start | bytes 1658884
  75.3 18.0 %copy-start.29 = (f32[180,16,2,4,1]{0,1,3,4,2:T(8,128)S(1)}, f32[180,16,2,4,1]{0,1,3,4,2:T(8,128)}, u32[]{:S(2)}) copy-start(f32[180,16,2,4,1]{0,1,3,4,2:T(8,128)} %constant.85) | copy-start | bytes 276484
  95.6 0.7 copy-start.21
  96.3 0.7 copy-start.27
  97.0 9.6 %copy-start.15 = (bf16[360,768]{1,0:T(8,128)(2,1)}, bf16[360,768]{1,0:T(8,128)(2,1)S(1)}, u32[]{:S(2)}) copy-start(bf16[360,768]{1,0:T(8,128)(2,1)S(1)} %reshape.337) | copy-start | bytes 1658884
  106.6 1.4 copy-start.30
  114.7 1.0 copy-start
  115.7 1.8 copy-start.2
  115.7 1.8 copy-start.18
  140.1 4.4 copy-start.6
  140.1 4.4 copy-start.12
  144.5 1.2 copy-start.13
  145.4 1.1 copy-start.5
  149.7 244.3 %reduce-scatter.3.cloned.1.call-start = ((), (), s32[]{:S(2)}) async-start(), calls=%async_computation.7 | async-start | bytes 4866048 | tf_op jit(solution)/shard_map/reduce_scatter | solution.py:136
  156.3 350.0 %reduce-scatter.5.cloned.1.call-start = ((), (), s32[]{:S(2)}) async-start(), calls=%async_computation.8 | async-start | bytes 4866048 | tf_op jit(solution)/shard_map/reduce_scatter | solution.py:127
  171.1 2.5 copy-start.23
  176.3 108.3 %all-to-all-start.4 = ((bf16[16,2,1,2,4,768]{5,3,4,1,2,0:T(2,128)(2,1)}), bf16[16,2,1,2,4,768]{5,3,4,1,2,0:T(2,128)(2,1)}, u32[]{:S(2)}, u32[]{:S(2)}) async-start(bf16[16,2,1,2,4,768]{5,3,4,1,2,0:T(2,128)(2,1)} %copy.129), calls=%async_computation.4 | async-start | bytes 786432 | tf_op jit(solution)/shard_map/all_to_all | solution.py:67
  281.8 2.7 copy-start.3
  281.8 2.7 copy-start.28
Sparse Core Ops, SparseCore 0:
  149.8 131.9 all-reduce.11
  287.3 106.6 reduce-scatter.2
  399.5 106.6 reduce-scatter.4
where the time goes:
time: 521 us; the launch traced here: 515 us
  waiting for transfers between devices  309 us (59%)
  matrix products  59.3 us (11%)
  blocking collectives  57.3 us (11%)
  local copies, waits for them, and re-layouts  31.9 us (6%)
  starting transfers between devices  22.8 us (4%)
  other arithmetic  19.5 us (4%)
  between operations  14.6 us (3%)
    reduce_scatter x1, waiting for transfers between devices, local(): lax.psum_scatter(term_two.astype(jnp.bfloat16), everyone, scatter_dimensi...  111 us
    psum x1, waiting for transfers between devices, local(): lax.psum((grad_gain_one, grad_gain_two, pulled[1], pulled[2], pulled[3],...  101 us
    reduce_scatter x1, waiting for transfers between devices, local(): lax.psum_scatter(term_one.astype(jnp.bfloat16), everyone, scatter_dimensi...  62 us
    psum x1, blocking collectives, local(): lax.psum((grad_gain_one, grad_gain_two, pulled[1], pulled[2], pulled[3],...  39.8 us
    all_to_all x3, waiting for transfers between devices, swap(): lax.all_to_all(pieces, 'space', split_axis=0, concat_axis=0, tiled=True)  22.8 us
    all_to_all x1, blocking collectives, swap(): lax.all_to_all(pieces, 'space', split_axis=0, concat_axis=0, tiled=True)  17.5 us
    dot_general x6, matrix products, block_dot(): return jnp.einsum('nri,nio->nro', values, weights, precision=high)  14.6 us
    all_to_all x3, starting transfers between devices, swap(): lax.all_to_all(pieces, 'space', split_axis=0, concat_axis=0, tiled=True)  14.5 us
  transfers between devices with their start and end apart: 7, of which 6 were waited for; matrix products, arithmetic and copies ran while one was open for 11% of the time, Pallas kernels for 0%

commit v1 on v0

--- a/solution.py
+++ b/solution.py
@@ -150,19 +150,18 @@
     grad_input = grad_mixed + grad_base
     bias_sum = jnp.sum(grad_hidden, axis=0)
     out_sum = jnp.sum(cotangent, axis=(0, 1, 2), dtype=jnp.float32)
-    totals = lax.psum(
-        (
-            grad_gain_one,
-            grad_gain_two,
-            pulled[1],
-            pulled[2],
-            pulled[3],
-            pulled[4],
-            bias_sum,
-            out_sum,
-        ),
-        everyone,
-    )
+    totals = (
+        grad_gain_one,
+        grad_gain_two,
+        pulled[1],
+        pulled[2],
+        pulled[3],
+        pulled[4],
+        bias_sum,
+        out_sum,
+    )
+    for i0 in ("space", "dp"):
+        totals = lax.psum(totals, i0)
     grad_scale = 1.0 / math.sqrt(samples * lax.axis_size("dp") * lat_total * lon_cells)
     return (
         grad_input,

time: 521 us -> 486 us (0.933)
  waiting for transfers between devices: 309 us -> 243 us
  blocking collectives: 57.3 us -> 86.5 us
    reduce_scatter x1, waiting for transfers between devices: 62 us -> 0.01 us  [local(): lax.psum_scatter(term_one.astype(jnp.bfloat16), everyone, scatter_dimensi...]
    psum x1 -> x2, blocking collectives: 39.8 us -> 69 us  [local(): totals = lax.psum(totals, i0)]
    all_to_all x3, waiting for transfers between devices: 22.8 us -> 34.6 us  [swap(): lax.all_to_all(pieces, 'space', split_axis=0, concat_axis=0, tiled=True)]
    reduce_scatter x1, waiting for transfers between devices: 111 us -> 100 us  [local(): lax.psum_scatter(term_two.astype(jnp.bfloat16), everyone, scatter_dimensi...]
    psum x1 -> x2, waiting for transfers between devices: 101 us -> 95 us  [local(): totals = lax.psum(totals, i0)]
  transfers between devices with their start and end apart: 7 -> 8, of which waited for: 6 -> 6; matrix products, arithmetic and copies ran while one was open for 11% -> 11% of each run, Pallas kernels for 0% -> 0%
where the time goes in v1:
time: 486 us; the launch traced here: 480 us
  waiting for transfers between devices  243 us (50%)
  blocking collectives  86.5 us (18%)
  matrix products  59.6 us (12%)
  local copies, waits for them, and re-layouts  32.4 us (7%)
  starting transfers between devices  22.9 us (5%)
  other arithmetic  19.3 us (4%)
  between operations  16.3 us (3%)
    reduce_scatter x1, waiting for transfers between devices, local(): lax.psum_scatter(term_two.astype(jnp.bfloat16), everyone, scatter_dimensi...  100 us
    psum x2, waiting for transfers between devices, local(): totals = lax.psum(totals, i0)  95 us
    psum x2, blocking collectives, local(): totals = lax.psum(totals, i0)  69 us
    all_to_all x3, waiting for transfers between devices, swap(): lax.all_to_all(pieces, 'space', split_axis=0, concat_axis=0, tiled=True)  34.6 us
    all_to_all x1, blocking collectives, swap(): lax.all_to_all(pieces, 'space', split_axis=0, concat_axis=0, tiled=True)  17.5 us
    dot_general x6, matrix products, block_dot(): return jnp.einsum('nri,nio->nro', values, weights, precision=high)  14.7 us
    all_to_all x3, starting transfers between devices, swap(): lax.all_to_all(pieces, 'space', split_axis=0, concat_axis=0, tiled=True)  14.6 us
    all_to_all x1, waiting for transfers between devices, local(): lax.all_to_all(stash, 'space', split_axis=1, concat_axis=0, tiled=True)  12.9 us
  transfers between devices with their start and end apart: 8, of which 6 were waited for; matrix products, arithmetic and copies ran while one was open for 11% of the time, Pallas kernels for 0%

profile of v1, /device:TPU:0, one launch (start us, length us, event | category | flops | bytes accessed | tf_op | source)
XLA Modules:
  0.0 480.0 jit_solution(2045607528156852707)
XLA Ops:
  8.0 7.4 %all-to-all-start = ((bf16[1,16,2,8640]{3,2,0,1:T(2,128)(2,1)}), bf16[1,16,2,8640]{3,2,0,1:T(2,128)(2,1)S(1)}, u32[]{:S(2)}, u32[]{:S(2)}) async-start(bf16[1,16,2,8640]{3,2,0,1:T(2,128)(2,1)} %bitcast.227), calls=%async_computation | async-start | bytes 1114112 | tf_op jit(solution)/shard_map/all_to_all | solution.py:108
  15.5 1.9 sort.17
  17.4 12.9 %all-to-all-done = bf16[1,16,2,8640]{3,2,0,1:T(2,128)(2,1)S(1)} async-done(((bf16[1,16,2,8640]{3,2,0,1:T(2,128)(2,1)}), bf16[1,16,2,8640]{3,2,0,1:T(2,128)(2,1)S(1)}, u32[]{:S(2)}, u32[]{:S(2)}) %all-to-all-start) | async-done | bytes 552992 | tf_op jit(solution)/shard_map/all_to_all | solution.py:108
  30.2 1.7 gather_fusion
  35.8 1.5 copy.105
  37.3 4.8 all-to-all-start.1
  42.7 0.9 copy.158
  43.6 1.9 fusion.71
  45.5 1.2 copy.161
  46.7 0.9 copy.160
  49.2 11.5 %all-to-all-done.1 = f32[16,2,1,2,4,768]{5,1,4,3,2,0:T(2,128)S(1)} async-done(((f32[16,2,1,2,4,768]{5,1,4,3,2,0:T(2,128)}), f32[16,2,1,2,4,768]{5,1,4,3,2,0:T(2,128)S(1)}, u32[]{:S(2)}, u32[]{:S(2)}) %all-to-all-start.1) | async-done | bytes 786464 | tf_op jit(solution)/shard_map/all_to_all | solution.py:67
  62.7 2.6 convolution_add_fusion.2
  65.3 1.4 convolution_add_fusion.1
  68.4 1.4 copy.118
  69.8 5.6 %all-to-all-start.2 = ((f32[16,2,1,2,4,768]{5,4,1,3,2,0:T(4,128)}), f32[16,2,1,2,4,768]{5,4,1,3,2,0:T(4,128)}, u32[]{:S(2)}, u32[]{:S(2)}) async-start(f32[16,2,1,2,4,768]{5,4,1,3,2,0:T(4,128)} %copy.118), calls=%async_computation.2 | async-start | bytes 1572864 | tf_op jit(solution)/shard_map/all_to_all | solution.py:67
  76.1 6.7 %fusion.75 = f32[360,3072]{1,0:T(8,128)} fusion(bf16[360,768]{1,0:T(8,128)(2,1)S(1)} %reshape.326, bf16[3072,768]{1,0:T(8,128)(2,1)} %param.30), kind=kOutput, calls=%fused_computation.144 | convolution fusion | flops 1698693120 | bytes 9695232 | tf_op jit(solution)/shard_map/td,fd->tf/dot_general | solution.py:130
  82.8 11.3 %all-to-all-done.2 = f32[16,2,1,2,4,768]{5,4,1,3,2,0:T(4,128)} async-done(((f32[16,2,1,2,4,768]{5,4,1,3,2,0:T(4,128)}), f32[16,2,1,2,4,768]{5,4,1,3,2,0:T(4,128)}, u32[]{:S(2)}, u32[]{:S(2)}) %all-to-all-start.2) | async-done | bytes 786464 | tf_op jit(solution)/shard_map/all_to_all | solution.py:67
  94.1 2.4 fusion.73
  97.8 9.6 %fusion.68 = (f32[3072]{0:T(1024)S(1)}, bf16[360,3072]{1,0:T(8,128)(2,1)S(1)}, f32[360,3072]{1,0:T(8,128)}) fusion(f32[360,3072]{1,0:T(8,128)} %fusion.75, f32[3072]{0:T(1024)S(1)} %copy-done.28, bf16[360,768]{1,0:T(8,128)(2,1)S(1)} %reshape.337, bf16[768,3072]{1,0:T(8,128)(2,1)} %param.28), kind=kOutput, calls=%fused_computation.138 | convolution fusion | flops 1723020288 | bytes 16355328 | tf_op jit(solution)/shard_map/dot_general | solution.py:122
  107.5 1.4 copy-done.30
  108.9 5.2 %fusion.23 = f32[360,768]{1,0:T(8,128)} fusion(bf16[768,3072]{1,0:T(8,128)(2,1)} %param.28, bf16[360,3072]{1,0:T(8,128)(2,1)S(1)} %get-tuple-element.78), kind=kOutput, calls=%fused_computation.58 | convolution fusion | flops 1698693120 | bytes 8036352 | tf_op jit(solution)/shard_map/tf,df->td/dot_general | solution.py:139
  114.1 1.4 reshape.338
  116.5 1.7 fusion.70
  119.2 17.5 %all_to_all.29 = bf16[16,2,1,2,4,768]{5,4,3,1,2,0:T(4,128)(2,1)S(1)} all-to-all(bf16[16,2,1,2,4,768]{5,4,3,1,2,0:T(4,128)(2,1)S(1)} %copy.120), channel_id=1, replica_groups=mesh['dp'=2,'space'=16] {'space'}, dimensions={0} | all-to-all | bytes 786432 | tf_op jit(solution)/shard_map/all_to_all | solution.py:67
  137.1 0.9 copy.122
  138.0 1.6 reshape.342
  139.6 1.3 copy.123
  140.9 4.4 fusion.74
  148.5 1.4 pad_add_fusion
  150.0 95.0 %all-reduce.15.cloned.1.call-done = (f32[2,8,96,96]{3,2,1,0:T(8,128)}, f32[2,8,96,96]{3,2,1,0:T(8,128)}) async-done(((f32[2,8,96,96]{3,2,1,0:T(8,128)}, f32[2,8,96,96]{3,2,1,0:T(8,128)}), (f32[2,8,96,96]{3,2,1,0:T(8,128)}, f32[2,8,96,96]{3,2,1,0:T(8,128)})) %all-reduce.15.cloned.1.call-update) | async-done | bytes 1179664 | tf_op jit(solution)/shard_map/psum | solution.py:164
  245.0 6.5 %convolution_convert_fusion.1 = bf16[3072,768]{1,0:T(8,128)(2,1)} fusion(bf16[360,768]{1,0:T(8,128)(2,1)} %copy-done.16, bf16[360,3072]{1,0:T(8,128)(2,1)} %copy-done.30), kind=kOutput, calls=%fused_computation.4 | convolution fusion | flops 1701052416 | bytes 7483392 | tf_op jit(solution)/shard_map/tf,td->fd/dot_general | solution.py:133
  251.9 7.6 %convolution_convert_fusion = bf16[3072,768]{1,0:T(8,128)(2,1)} fusion(bf16[360,768]{1,0:T(8,128)(2,1)} %copy-done.15, f32[360,3072]{1,0:T(8,128)} %get-tuple-element.97), kind=kOutput, calls=%fused_computation.3 | convolution fusion | flops 1711005696 | bytes 9695232 | tf_op jit(solution)/shard_map/tf,td->fd/dot_general | solution.py:126
  259.4 4.6 fusion.21
  264.1 2.5 copy.126
  266.5 2.5 reshape.345
  269.0 1.7 fusion.14
  270.7 1.0 copy.129
  271.7 4.3 all-to-all-start.4
  276.4 11.8 %all-to-all-done.4 = bf16[16,2,1,2,4,768]{5,3,4,1,2,0:T(2,128)(2,1)} async-done(((bf16[16,2,1,2,4,768]{5,3,4,1,2,0:T(2,128)(2,1)}), bf16[16,2,1,2,4,768]{5,3,4,1,2,0:T(2,128)(2,1)}, u32[]{:S(2)}, u32[]{:S(2)}) %all-to-all-start.4) | async-done | bytes 393248 | tf_op jit(solution)/shard_map/all_to_all | solution.py:67
  288.2 2.2 multiply_reduce_fusion.2
  292.1 2.1 copy.132
  294.2 60.5 %all-reduce.8 = (f32[3072]{0:T(1024)S(1)}, f32[768]{0:T(1024)S(1)}, f32[768]{0:T(1024)S(1)}, f32[768]{0:T(1024)S(1)}, f32[2,768]{1,0:T(2,128)S(1)}, /*index=5*/f32[2,768]{1,0:T(2,128)S(1)}) all-reduce(f32[3072]{0:T(1024)S(1)} %get-tuple-element.77, f32[768]{0:T(1024)S(1)} %get-tuple-element.93, ...), channel_id=1, replica_groups=mesh['dp'=2,'space'=16] {'space'}, use_global_device_ids=true, to_apply=%region_12.13 | all-reduce | flops 8448 | bytes 67584 | tf_op jit(solution)/shard_map/psum | solution.py:164
  354.7 8.5 %all-reduce.10 = (f32[3072]{0:T(1024)S(1)}, f32[768]{0:T(1024)S(1)}, f32[768]{0:T(1024)S(1)}, f32[768]{0:T(1024)S(1)}, f32[2,768]{1,0:T(2,128)S(1)}, /*index=5*/f32[2,768]{1,0:T(2,128)S(1)}) all-reduce(f32[3072]{0:T(1024)S(1)} %get-tuple-element.61, f32[768]{0:T(1024)S(1)} %get-tuple-element.62, ...), channel_id=1, replica_groups=mesh['dp'=2,'space'=16] {'dp'}, use_global_device_ids=true, to_apply=%region_13.14 | all-reduce | flops 8448 | bytes 67584 | tf_op jit(solution)/shard_map/psum | solution.py:164
  365.6 2.2 broadcast_multiply_fusion.1
  367.8 1.0 broadcast_multiply_fusion
  368.7 1.6 multiply_bitcast_fusion
  370.4 100.3 %reduce-scatter.5.cloned.1.call-done = bf16[96,768]{1,0:T(8,128)(2,1)} async-done(((bf16[3072,768]{1,0:T(8,128)(2,1)}), bf16[96,768]{1,0:T(8,128)(2,1)}) %reduce-scatter.5.cloned.1.call-update) | async-done | bytes 147472 | tf_op jit(solution)/shard_map/reduce_scatter | solution.py:127
  470.7 1.6 convert_multiply_fusion
  (131 shorter events, 21.9 us)
Async XLA Ops:
  8.0 22.2 %all-to-all-start = ((bf16[1,16,2,8640]{3,2,0,1:T(2,128)(2,1)}), bf16[1,16,2,8640]{3,2,0,1:T(2,128)(2,1)S(1)}, u32[]{:S(2)}, u32[]{:S(2)}) async-start(bf16[1,16,2,8640]{3,2,0,1:T(2,128)(2,1)} %bitcast.227), calls=%async_computation | async-start | bytes 1114112 | tf_op jit(solution)/shard_map/all_to_all | solution.py:108
  34.3 0.9 copy-start.20
  34.3 0.9 copy-start.23
  37.3 4.8 copy-start.26
  37.3 5.0 %copy-start.27 = (f32[2,768]{1,0:T(2,128)S(1)}, f32[2,768]{1,0:T(2,128)}, u32[]{:S(2)}) copy-start(f32[2,768]{1,0:T(2,128)} %param.26) | copy-start | bytes 18436
  37.3 5.1 %copy-start.10 = (f32[2,8,96,96]{3,2,1,0:T(8,128)S(1)}, f32[2,8,96,96]{3,2,1,0:T(8,128)}, u32[]{:S(2)}) copy-start(f32[2,8,96,96]{3,2,1,0:T(8,128)} %param.23) | copy-start | bytes 1769476
  37.3 23.4 %all-to-all-start.1 = ((f32[16,2,1,2,4,768]{5,1,4,3,2,0:T(2,128)}), f32[16,2,1,2,4,768]{5,1,4,3,2,0:T(2,128)S(1)}, u32[]{:S(2)}, u32[]{:S(2)}) async-start(f32[16,2,1,2,4,768]{5,1,4,3,2,0:T(2,128)} %copy.105), calls=%async_computation.1 | async-start | bytes 1572864 | tf_op jit(solution)/shard_map/all_to_all | solution.py:67
  42.7 19.9 %copy-start.7 = (f32[1,8,96,96]{2,3,1,0:T(8,128)}, f32[1,8,96,96]{2,3,1,0:T(8,128)S(1)}, u32[]{:S(2)}) copy-start(f32[1,8,96,96]{2,3,1,0:T(8,128)S(1)} %copy.159) | copy-start | bytes 884740
  46.7 2.5 copy-start.8
  46.7 14.0 %copy-start.21 = (f32[16,2,16,2,1,1]{0,2,1,3,5,4:T(8,128)S(1)}, f32[16,2,16,2,1,1]{0,2,1,3,5,4:T(8,128)}, u32[]{:S(2)}) copy-start(f32[16,2,16,2,1,1]{0,2,1,3,5,4:T(8,128)} %constant.86) | copy-start | bytes 12292
  62.6 2.6 copy-start.4
  62.6 2.6 copy-start.9
  62.6 2.6 copy-start.17
  62.6 2.6 copy-start.18
  65.2 1.4 copy-start.13
  67.1 0.8 copy-start.25
  69.7 6.1 %copy-start.1 = (bf16[2,1,180,768]{3,0,2,1:T(2,128)(2,1)S(1)}, bf16[2,1,180,768]{3,0,2,1:T(2,128)(2,1)}, u32[]{:S(2)}) copy-start(bf16[2,1,180,768]{3,0,2,1:T(2,128)(2,1)} %param.31) | copy-start | bytes 1658884
  69.8 24.3 %all-to-all-start.2 = ((f32[16,2,1,2,4,768]{5,4,1,3,2,0:T(4,128)}), f32[16,2,1,2,4,768]{5,4,1,3,2,0:T(4,128)}, u32[]{:S(2)}, u32[]{:S(2)}) async-start(f32[16,2,1,2,4,768]{5,4,1,3,2,0:T(4,128)} %copy.118), calls=%async_computation.2 | async-start | bytes 1572864 | tf_op jit(solution)/shard_map/all_to_all | solution.py:67
  75.3 169.7 %all-reduce.15.cloned.1.call-start = ((), (), s32[]{:S(2)}) async-start(), calls=%async_computation.9 | async-start | bytes 3145728 | tf_op jit(solution)/shard_map/psum | solution.py:164
  76.1 6.7 %copy-start.15 = (bf16[360,768]{1,0:T(8,128)(2,1)}, bf16[360,768]{1,0:T(8,128)(2,1)S(1)}, u32[]{:S(2)}) copy-start(bf16[360,768]{1,0:T(8,128)(2,1)S(1)} %reshape.326) | copy-start | bytes 1658884
  76.1 18.0 %copy-start.29 = (f32[180,16,2,4,1]{0,1,3,4,2:T(8,128)S(1)}, f32[180,16,2,4,1]{0,1,3,4,2:T(8,128)}, u32[]{:S(2)}) copy-start(f32[180,16,2,4,1]{0,1,3,4,2:T(8,128)} %constant.85) | copy-start | bytes 276484
  96.4 0.7 copy-start.22
  97.1 0.7 copy-start.28
  97.8 9.6 %copy-start.16 = (bf16[360,768]{1,0:T(8,128)(2,1)}, bf16[360,768]{1,0:T(8,128)(2,1)S(1)}, u32[]{:S(2)}) copy-start(bf16[360,768]{1,0:T(8,128)(2,1)S(1)} %reshape.337) | copy-start | bytes 1658884
  107.5 1.4 copy-start.30
  115.5 1.0 copy-start
  116.5 1.8 copy-start.2
  116.5 1.8 copy-start.19
  140.9 4.4 copy-start.6
  140.9 4.4 copy-start.14
  145.3 1.2 copy-start.12
  146.2 1.1 copy-start.5
  149.9 215.7 %all-reduce.17.cloned.1.call-start = ((), (), s32[]{:S(2)}) async-start(), calls=%async_computation.10 | async-start | bytes 3145728 | tf_op jit(solution)/shard_map/psum | solution.py:164
  245.0 123.7 %reduce-scatter.3.cloned.1.call-start = ((), (), s32[]{:S(2)}) async-start(), calls=%async_computation.7 | async-start | bytes 4866048 | tf_op jit(solution)/shard_map/reduce_scatter | solution.py:136
  251.6 219.1 %reduce-scatter.5.cloned.1.call-start = ((), (), s32[]{:S(2)}) async-start(), calls=%async_computation.8 | async-start | bytes 4866048 | tf_op jit(solution)/shard_map/reduce_scatter | solution.py:127
  266.5 2.5 copy-start.24
  271.7 16.5 %all-to-all-start.4 = ((bf16[16,2,1,2,4,768]{5,3,4,1,2,0:T(2,128)(2,1)}), bf16[16,2,1,2,4,768]{5,3,4,1,2,0:T(2,128)(2,1)}, u32[]{:S(2)}, u32[]{:S(2)}) async-start(bf16[16,2,1,2,4,768]{5,3,4,1,2,0:T(2,128)(2,1)} %copy.129), calls=%async_computation.4 | async-start | bytes 786432 | tf_op jit(solution)/shard_map/all_to_all | solution.py:67
  290.5 1.1 copy-start.3
  365.6 2.2 copy-start.11
Sparse Core Ops, SparseCore 0:
  150.0 94.8 all-reduce.14
  247.3 50.5 all-reduce.16
Sparse Core Ops, SparseCore 1:
  251.7 106.9 reduce-scatter.2
  364.0 106.7 reduce-scatter.4
